TPU v7x, 32 devices: a whole 2x2x4 slice. The times are simulated.
32 devices in a mesh: lat: 4 (over z), fld: 4 (over y, x), rep: 2 (over core).
Axes of the slice: x: 2, y: 2, z: 4, core: 2. Of those that a mesh axis runs over, the one named last changes fastest.
Arguments:
- field: float32 [12, 1280, 2560], P('fld', ('lat', 'rep')), may hold values from -6 to 6
- wind_zonal: float32 [12, 1280, 2560], P('fld', ('lat', 'rep')), may hold values from -4 to 4
- wind_merid: float32 [12, 1280, 2560], P('fld', ('lat', 'rep')), may hold values from -4 to 4
- band: int32 [12, 2], replicated, may hold values from 0 to 1280, as said below
- waves: int32 [16, 80], replicated, may hold values from -1 to 1279, as said below
- legendre: bfloat16 [16, 1280, 51328], P(('lat', 'fld')), may hold values from -0.15625 to 0.15625
Outputs:
- spectrum: float32 [16, 12, 2, 51328], P(('lat', 'fld'), 'rep')
Inputs may be any that keep to these rules, and one draw needn't show every extreme that they name: band[f, 0] is below 320 and band[f, 1] is above 960, for every field-level. `waves`: every wavenumber 0 to 1279 stands in exactly one slot of one group; -1 marks an empty slot. Wavenumber m takes 1280 - m columns, and the wavenumbers of one group take at most 51240 columns together; some group takes exactly 51240.
All inputs are finite; a program needn't handle non-finite values.
Results may differ from a plain program's by a relative error of at most 0.0056.
Values may be sent and summed in bfloat16 or wider, within the bound.
A program may use at most 256 MiB of HBM per device.

v0:
```python
import math

import jax
import jax.numpy as jnp
from jax import lax
from jax.sharding import PartitionSpec as P

M = 1280


def with_halo(value, sides, width):
    for axis, dim in sides:
        peers, length = (lax.axis_size(axis), value.shape[dim])
        up = [(i, (i + 1) % peers) for i in range(peers - 1)]
        down = [(j, i) for i, j in up]
        last = lax.slice_in_dim(value, length - width, length, axis=dim)
        first = lax.slice_in_dim(value, 0, width, axis=dim)
        before = lax.ppermute(last, axis, up)
        after = lax.ppermute(first, axis, down)
        value = jnp.concatenate([before, value, after], axis=dim)
    return value


def dft_matrix(lon_count, wave_count):
    lon_ids = lax.broadcasted_iota(jnp.int32, (lon_count, wave_count), 0)
    wave_ids = lax.broadcasted_iota(jnp.int32, (lon_count, wave_count), 1)
    angles = (lon_ids * wave_ids % lon_count).astype(jnp.float32) * (2.0 * math.pi / lon_count)
    scaling = 1.0 / math.sqrt(lon_count)
    return jnp.concatenate([jnp.cos(angles) * scaling, -jnp.sin(angles) * scaling], axis=1).astype(
        jnp.bfloat16
    )


def tendency(centre, above_row, below_row, zonal_wind, merid_wind):
    eastward = jnp.roll(centre, -1, axis=-1)
    westward = jnp.roll(centre, 1, axis=-1)
    return (
        -(zonal_wind + centre) * (eastward - westward) * 0.5
        - merid_wind * (above_row - below_row) * 0.5
    )


def band_mask(bounds, first_row, row_total):
    row_ids = first_row + lax.broadcasted_iota(jnp.int32, (1, row_total, 1), 1)
    lower_edge = bounds[:, 0][:, None, None]
    upper_edge = bounds[:, 1][:, None, None]
    return ((row_ids >= lower_edge) & (row_ids < upper_edge)).astype(jnp.float32)


def body(field, wind_zonal, wind_merid, band, waves, legendre):
    field_count, row_count, lon_count = field.shape
    lat_size = lax.axis_size("lat")
    fld_size = lax.axis_size("fld")
    rep_size = lax.axis_size("rep")
    first_row = (lax.axis_index("lat") * rep_size + lax.axis_index("rep")) * row_count
    bounds = lax.dynamic_slice_in_dim(band, lax.axis_index("fld") * field_count, field_count, 0)
    in_band = band_mask(bounds, first_row, row_count)
    padded = with_halo(field, ((("lat", "rep"), 1),), 1)
    first_section = field + in_band * tendency(
        field, padded[:, 2:], padded[:, :-2], wind_zonal, wind_merid
    )
    padded_section = with_halo(first_section, ((("lat", "rep"), 1),), 1)
    advected = 0.5 * (
        field
        + first_section
        + in_band
        * tendency(
            first_section, padded_section[:, 2:], padded_section[:, :-2], wind_zonal, wind_merid
        )
    )
    grid_low = advected.astype(jnp.bfloat16)
    spectra = jnp.dot(
        grid_low.reshape(field_count * row_count, lon_count),
        dft_matrix(lon_count, M),
        preferred_element_type=jnp.float32,
    ).astype(jnp.bfloat16)
    spectra = spectra.reshape(field_count, row_count, 2, M)
    slot_count = waves.shape[1]
    wave_index = jnp.where(waves >= 0, waves, 0)
    picked = jnp.take(spectra, wave_index.reshape(-1), axis=3)
    picked = picked.reshape(field_count, row_count, 2, lat_size, fld_size, slot_count)
    outgoing = jnp.transpose(picked, (5, 2, 4, 0, 3, 1)).reshape(
        slot_count, 2, fld_size * field_count, lat_size * row_count
    )
    received = lax.all_to_all(
        lax.all_to_all(outgoing, "lat", split_axis=3, concat_axis=3, tiled=True),
        "fld",
        split_axis=2,
        concat_axis=2,
        tiled=True,
    )
    group = lax.axis_index("lat") * fld_size + lax.axis_index("fld")
    own_waves = lax.dynamic_index_in_dim(waves, group, 0, keepdims=False)
    counts = jnp.where(own_waves >= 0, M - own_waves, 0)
    offsets = jnp.cumsum(counts) - counts
    col_count = legendre.shape[2]
    col_ids = lax.broadcasted_iota(jnp.int32, (slot_count, col_count), 1)
    segments = ((col_ids >= offsets[:, None]) & (col_ids < (offsets + counts)[:, None])).astype(
        jnp.float32
    )
    total_fields = fld_size * field_count
    regrouped = lax.all_to_all(received, "rep", split_axis=2, concat_axis=3, tiled=True)
    half_fields = total_fields // rep_size
    ordered = regrouped.reshape(slot_count, 2, half_fields, rep_size, lat_size, row_count)
    ordered = jnp.transpose(ordered, (0, 1, 2, 4, 3, 5)).reshape(
        slot_count * 2 * half_fields, rep_size * lat_size * row_count
    )
    products = jnp.dot(ordered, legendre[0], preferred_element_type=jnp.float32)
    spectrum = jnp.einsum(
        "scfk,sk->fck", products.reshape(slot_count, 2, half_fields, col_count), segments
    )
    return spectrum[None]


def solution(mesh):
    placed = (
        P("fld", ("lat", "rep"), None),
        P("fld", ("lat", "rep"), None),
        P("fld", ("lat", "rep"), None),
        P(),
        P(),
        P(("lat", "fld"), None, None),
    )
    return jax.shard_map(
        body,
        mesh=mesh,
        in_specs=placed,
        out_specs=P(("lat", "fld"), "rep", None, None),
        check_vma=False,
    )
```

profile of v0, /device:TPU:0, one launch (start us, length us, event | category | flops | bytes accessed | tf_op | source)
XLA Modules:
  0.0 497.4 jit_solution(12146686982743537627)
XLA Ops:
  0.0 1.1 fusion.46
  1.1 1.3 collective-permute-start
  2.4 3.0 collective-permute-start.1
  5.5 1.2 fusion.44
  6.7 9.0 %fusion.45 = (f32[3,160,2559]{2,1,0:T(8,128)}, f32[3,160,2559]{2,1,0:T(8,128)}) fusion(f32[3,160,2560]{2,1,0:T(8,128)} %param.6), kind=kLoop, calls=%fused_computation.69 | loop fusion | bytes 19653120 | tf_op jit(solution)/shard_map/jit(_roll_static)/slice | solution.py:36
  15.7 56.0 %multiply_convert_fusion = (bf16[2560,1280]{1,0:T(8,128)(2,1)}, bf16[2560,1280]{1,0:T(8,128)(2,1)}) fusion(), kind=kLoop, calls=%fused_computation.16 | loop fusion | flops 45875200 | bytes 13107200 | tf_op jit(solution)/shard_map/convert.1
  72.0 0.2 copy.24
  72.2 14.0 %fusion.29 = f32[3,160,2560]{2,1,0:T(8,128)S(1)} fusion(f32[3,160,2560]{2,1,0:T(8,128)} %param.6, f32[3,160,2560]{2,1,0:T(8,128)} %param.8, f32[3,1,2560]{2,1,0:T(1,128)S(1)} %collective-permute-done.1, f32[3,1,2560]{2,1,0:T(1,128)S(1)} %collective-permute-done, f32[3,160,1]{2,1,0:T(8,128)S(1)} %get-tuple-element.12, f32[3,160,2559]{2,1,0:T(8,128)} %get-tuple-element.14, ...), kind=kLoop, calls=%fused_computation.38 | loop fusion | flops 18432000 | bytes 29554560 | tf_op jit(solution)/shard_map/add | solution.py:59
  86.2 4.1 fusion.42
  90.4 1.3 collective-permute-start.2
  91.6 5.4 %collective-permute-start.3 = (f32[3,1,2560]{2,1,0:T(1,128)S(1)}, f32[3,1,2560]{2,1,0:T(1,128)S(1)}, u32[]{:S(2)}, u32[]{:S(2)}) collective-permute-start(f32[3,1,2560]{2,1,0:T(1,128)S(1)} %get-tuple-element.10), channel_id=1, source_target_pairs={{0,1},{1,8},{8,9},{9,16},{16,17},{17,24},{24,25},{2,3},{3,10},{10,... | collective-permute-start | bytes 92168 | tf_op jit(solution)/shard_map/ppermute | solution.py:18
  97.2 0.5 collective-permute-done.3
  97.7 7.8 %fusion.23 = bf16[3,160,2560]{2,1,0:T(8,128)(2,1)S(1)} fusion(f32[3,160,2560]{2,1,0:T(8,128)} %param.8, f32[3,160,2560]{2,1,0:T(8,128)S(1)} %fusion.29, f32[3,1,2560]{2,1,0:T(1,128)S(1)} %collective-permute-done.3, f32[3,1,2560]{2,1,0:T(1,128)S(1)} %collective-permute-done.2, f32[3,160,1]{2,1,0:T(8,128)S(1)} %get-tuple-element.6, ...), kind=kLoop, calls=%fused_computation.30 | loop fusion | flops 22118400 | bytes 32012160 | tf_op jit(solution)/shard_map/convert_element_type | solution.py:71
  105.5 12.7 %fusion.34 = bf16[480,2560]{1,0:T(8,128)(2,1)} fusion(bf16[480,2560]{1,0:T(8,128)(2,1)S(1)} %bitcast.54, bf16[2560,1280]{1,0:T(8,128)(2,1)} %get-tuple-element.19, bf16[2560,1280]{1,0:T(8,128)(2,1)} %get-tuple-element.20), kind=kOutput, calls=%fused_computation.46 | convolution fusion | flops 6318899200 | bytes 18022400 | tf_op jit(solution)/shard_map/dot_general | solution.py:72
  118.2 5.2 %reshape.195 = bf16[3,160,2,1280]{3,2,1,0:T(2,128)(2,1)S(1)} reshape(bf16[480,2560]{1,0:T(8,128)(2,1)} %fusion.34) | data formatting | bytes 4915200 | tf_op jit(solution)/shard_map/reshape | solution.py:77
  123.4 11.6 %copy.25 = bf16[3,160,2,1280]{1,2,3,0:T(2,128)(2,1)} copy(bf16[3,160,2,1280]{3,2,1,0:T(2,128)(2,1)S(1)} %reshape.195) | data formatting | bytes 4915200 | tf_op jit(solution)/shard_map/reshape | solution.py:77
  135.0 15.2 %gather_fusion = bf16[1280,3,160,2]{2,3,1,0:T(2,128)(2,1)} fusion(bf16[3,160,2,1280]{1,2,3,0:T(2,128)(2,1)} %copy.25, s32[2048]{0:T(1024)S(1)} %pad_clamp_fusion), kind=kCustom, calls=%fused_computation | custom fusion | bytes 4920320 | tf_op jit(solution)/shard_map/jit(_take)/gather | solution.py:80
  150.2 11.6 %fusion.37 = bf16[80,2,4,3,4,160]{5,4,0,3,2,1:T(4,128)(2,1)} fusion(bf16[3,160,2,4,4,80]{1,2,0,5,4,3:T(2,128)(2,1)} %bitcast.52, pred[4,4,80]{0,2,1:T(8,128)(4,1)S(1)} %copy.24), kind=kLoop, calls=%fused_computation.48 | loop fusion | flops 1228800 | bytes 4916480 | tf_op jit(solution)/shard_map/transpose | solution.py:82
  161.8 16.7 %copy.40 = bf16[80,2,4,3,4,160]{0,1,3,2,5,4:T(2,128)(2,1)} copy(bf16[80,2,4,3,4,160]{5,4,0,3,2,1:T(4,128)(2,1)} %fusion.37) | data formatting | bytes 4915200 | tf_op jit(solution)/shard_map/reshape | solution.py:82
  178.5 7.4 %all-to-all-start = ((bf16[80,2,12,640]{0,1,2,3:T(2,128)(2,1)}), bf16[80,2,12,640]{0,1,2,3:T(2,128)(2,1)}, u32[]{:S(2)}, u32[]{:S(2)}) async-start(bf16[80,2,12,640]{0,1,2,3:T(2,128)(2,1)} %bitcast.50), calls=%async_computation | async-start | bytes 7864320 | tf_op jit(solution)/shard_map/all_to_all | solution.py:86
  186.3 87.0 %all-to-all-done = bf16[80,2,12,640]{0,1,2,3:T(2,128)(2,1)} async-done(((bf16[80,2,12,640]{0,1,2,3:T(2,128)(2,1)}), bf16[80,2,12,640]{0,1,2,3:T(2,128)(2,1)}, u32[]{:S(2)}, u32[]{:S(2)}) %all-to-all-start) | async-done | bytes 2457632 | tf_op jit(solution)/shard_map/all_to_all | solution.py:86
  273.2 8.8 %copy.28 = bf16[80,2,12,640]{3,0,1,2:T(8,128)(2,1)} copy(bf16[80,2,12,640]{0,1,2,3:T(2,128)(2,1)} %all-to-all-done) | data formatting | bytes 4915200 | tf_op jit(solution)/shard_map/all_to_all | solution.py:86
  282.1 3.7 all-to-all-start.1
  285.8 7.9 %fusion.6 = f32[51328,80]{0,1:T(8,128)} fusion(s32[80]{0:T(128)S(1)} %reduce.1, s32[80]{0:T(128)S(1)} %bitcast_subtract_fusion), kind=kLoop, calls=%fused_computation.9 | loop fusion | flops 16424960 | bytes 16425600
  293.6 20.3 %all-to-all-done.1 = bf16[80,2,12,640]{3,0,1,2:T(8,128)(2,1)S(1)} async-done(((bf16[80,2,12,640]{3,0,1,2:T(8,128)(2,1)}), bf16[80,2,12,640]{3,0,1,2:T(8,128)(2,1)S(1)}, u32[]{:S(2)}, u32[]{:S(2)}) %all-to-all-start.1) | async-done | bytes 2457632 | tf_op jit(solution)/shard_map/all_to_all | solution.py:85
  314.0 5.7 %all_to_all.25 = bf16[80,2,12,640]{3,0,1,2:T(8,128)(2,1)S(1)} all-to-all(bf16[80,2,12,640]{3,0,1,2:T(8,128)(2,1)S(1)} %all-to-all-done.1), channel_id=1, replica_groups=mesh['lat'=4,'fld'=4,'rep'=2] {'rep'}, dimensions={2} | all-to-all | bytes 4915200 | tf_op jit(solution)/shard_map/all_to_all | solution.py:102
  319.6 0.2 copy.30
  319.9 4.4 reshape.198
  324.2 10.1 %copy.31 = bf16[80,2,6,4,2,160]{5,4,3,0,2,1:T(2,128)(2,1)} copy(bf16[80,2,6,4,2,160]{5,3,0,4,2,1:T(4,128)(2,1)} %bitcast.51) | data formatting | bytes 4915200 | tf_op jit(solution)/shard_map/transpose | solution.py:105
  334.3 7.0 %dot_general.12 = bf16[80,2,6,1280]{3,0,2,1:T(8,128)(2,1)} reshape(bf16[80,2,6,4,2,160]{5,4,3,0,2,1:T(2,128)(2,1)} %copy.31) | data formatting | bytes 4915200 | tf_op jit(solution)/shard_map/dot_general | solution.py:108
  341.4 152.9 %multiply_reduce_fusion = f32[51328,2,6]{0,2,1:T(8,128)S(1)} fusion(f32[51328,80]{0,1:T(8,128)} %fusion.6, bf16[80,2,6,1280]{3,0,2,1:T(8,128)(2,1)} %dot_general.12, bf16[1,1280,51328]{2,1,0:T(8,128)(2,1)} %param.11), kind=kOutput, calls=%fused_computation.1 | convolution fusion | flops 126241628160 | bytes 152745984 | tf_op jit(solution)/shard_map/dot_general | solution.py:108
  494.3 2.7 copy.47
  (30 shorter events, 0.8 us)
Async XLA Ops:
  0.0 71.7 %copy-start = (s32[12,2]{0,1:T(2,128)S(1)}, s32[12,2]{0,1:T(2,128)}, u32[]{:S(2)}) copy-start(s32[12,2]{0,1:T(2,128)} %param.9) | copy-start | bytes 292
  1.1 71.1 %collective-permute-start = (f32[3,1,2560]{2,1,0:T(1,128)S(1)}, f32[3,1,2560]{2,1,0:T(1,128)S(1)}, u32[]{:S(2)}, u32[]{:S(2)}) collective-permute-start(f32[3,1,2560]{2,1,0:T(1,128)S(1)} %get-tuple-element.15), channel_id=1, source_target_pairs={{1,0},{8,1},{9,8},{16,9},{17,16},{24,17},{25,24},{3,2},{10,3},{11,... | collective-permute-start | bytes 92168 | tf_op jit(solution)/shard_map/ppermute | solution.py:19
  2.4 69.8 %collective-permute-start.1 = (f32[3,1,2560]{2,1,0:T(1,128)S(1)}, f32[3,1,2560]{2,1,0:T(1,128)S(1)}, u32[]{:S(2)}, u32[]{:S(2)}) collective-permute-start(f32[3,1,2560]{2,1,0:T(1,128)S(1)} %get-tuple-element.16), channel_id=1, source_target_pairs={{0,1},{1,8},{8,9},{9,16},{16,17},{17,24},{24,25},{2,3},{3,10},{10,... | collective-permute-start | bytes 92168 | tf_op jit(solution)/shard_map/ppermute | solution.py:18
  15.7 56.1 %copy-start.2 = (s32[16,80]{1,0:T(8,128)S(1)}, s32[16,80]{1,0:T(8,128)}, u32[]{:S(2)}) copy-start(s32[16,80]{1,0:T(8,128)} %param.10) | copy-start | bytes 15364
  15.7 82.0 %slice-start = ((s8[4915200]{0:T(1024)(128)(4,1)}), s8[720896]{0:T(1024)(128)(4,1)S(1)}, s32[]{:S(2)}) async-start(s8[4915200]{0:T(1024)(128)(4,1)} %bitcast.48), calls=%async_computation.3 | async-start | bytes 1441792
  72.2 25.5 %slice-start.1 = ((s8[4915200]{0:T(1024)(128)(4,1)}), s8[4194304]{0:T(1024)(128)(4,1)S(1)}, s32[]{:S(2)}) async-start(s8[4915200]{0:T(1024)(128)(4,1)} %bitcast.48), calls=%async_computation.4 | async-start | bytes 8388608
  90.4 6.8 %collective-permute-start.2 = (f32[3,1,2560]{2,1,0:T(1,128)S(1)}, f32[3,1,2560]{2,1,0:T(1,128)S(1)}, u32[]{:S(2)}, u32[]{:S(2)}) collective-permute-start(f32[3,1,2560]{2,1,0:T(1,128)S(1)} %get-tuple-element.9), channel_id=1, source_target_pairs={{1,0},{8,1},{9,8},{16,9},{17,16},{24,17},{25,24},{3,2},{10,3},{11,... | collective-permute-start | bytes 92168 | tf_op jit(solution)/shard_map/ppermute | solution.py:19
  91.6 6.1 %collective-permute-start.3 = (f32[3,1,2560]{2,1,0:T(1,128)S(1)}, f32[3,1,2560]{2,1,0:T(1,128)S(1)}, u32[]{:S(2)}, u32[]{:S(2)}) collective-permute-start(f32[3,1,2560]{2,1,0:T(1,128)S(1)} %get-tuple-element.10), channel_id=1, source_target_pairs={{0,1},{1,8},{8,9},{9,16},{16,17},{17,24},{24,25},{2,3},{3,10},{10,... | collective-permute-start | bytes 92168 | tf_op jit(solution)/shard_map/ppermute | solution.py:18
  178.5 94.7 %all-to-all-start = ((bf16[80,2,12,640]{0,1,2,3:T(2,128)(2,1)}), bf16[80,2,12,640]{0,1,2,3:T(2,128)(2,1)}, u32[]{:S(2)}, u32[]{:S(2)}) async-start(bf16[80,2,12,640]{0,1,2,3:T(2,128)(2,1)} %bitcast.50), calls=%async_computation | async-start | bytes 7864320 | tf_op jit(solution)/shard_map/all_to_all | solution.py:86
  282.1 31.9 %all-to-all-start.1 = ((bf16[80,2,12,640]{3,0,1,2:T(8,128)(2,1)}), bf16[80,2,12,640]{3,0,1,2:T(8,128)(2,1)S(1)}, u32[]{:S(2)}, u32[]{:S(2)}) async-start(bf16[80,2,12,640]{3,0,1,2:T(8,128)(2,1)} %copy.28), calls=%async_computation.1 | async-start | bytes 4915200 | tf_op jit(solution)/shard_map/all_to_all | solution.py:85
  341.4 155.6 %copy-start.1 = (s32[12,2]{0,1:T(2,128)S(1)}, s32[12,2]{0,1:T(2,128)}, u32[]{:S(2)}) copy-start(s32[12,2]{0,1:T(2,128)} %param.9) | copy-start | bytes 292
where the time goes:
time: 504 us; the launch traced here: 497 us
  matrix products  166 us (33%)
  waiting for transfers between devices  108 us (21%)
  local copies, waits for them, and re-layouts  98 us (19%)
  other arithmetic  97.7 us (19%)
  starting transfers between devices  22.1 us (4%)
  blocking collectives  5.68 us (1%)
    dot_general x1, matrix products, body(): products = jnp.dot(ordered, legendre[0], preferred_element_type=jnp.float32)  153 us
    all_to_all x1, waiting for transfers between devices, body(): lax.all_to_all(outgoing, 'lat', split_axis=3, concat_axis=3, tiled=True)  87 us
    another operation x3, other arithmetic  56.3 us
    all_to_all x1, waiting for transfers between devices, body(): lax.all_to_all(lax.all_to_all(outgoing, 'lat', split_axis=3, concat_axis=...  20.3 us
    reshape x2, local copies, waits for them, and re-layouts, body(): spectra = spectra.reshape(field_count, row_count, 2, M)  16.8 us
    reshape x1, local copies, waits for them, and re-layouts, body(): jnp.transpose(picked, (5, 2, 4, 0, 3, 1))  16.7 us
    gather x1, local copies, waits for them, and re-layouts, body(): picked = jnp.take(spectra, wave_index.reshape(-1), axis=3)  15.2 us
    slice x4, local copies, waits for them, and re-layouts, tendency(): westward = jnp.roll(centre, 1, axis=-1)  14.4 us
  transfers between devices with their start and end apart: 6, of which 3 were waited for; matrix products, arithmetic and copies ran while one was open for 15% of the time, Pallas kernels for 0%

commit v1 on v0

--- a/solution.py
+++ b/solution.py
@@ -1,11 +1,17 @@
+import functools
 import math
 
 import jax
 import jax.numpy as jnp
 from jax import lax
+from jax.experimental import pallas as pl
+from jax.experimental.pallas import tpu as pltpu
 from jax.sharding import PartitionSpec as P
 
 M = 1280
+LANES = 128
+WINDOW = 16
+TILE = 1024
 
 
 def with_halo(value, sides, width):
@@ -47,6 +53,204 @@
     return ((row_ids >= lower_edge) & (row_ids < upper_edge)).astype(jnp.float32)
 
 
+def transform_kernel(lon_count, table_ref, grid_ref, out_ref, matrix):
+    slots = table_ref.shape[1]
+    low_cos, low_sin = table_ref[0], table_ref[1]
+    high_cos, high_sin = table_ref[2], table_ref[3]
+    for part in range(lon_count // LANES):
+        columns = slice(part * LANES, (part + 1) * LANES)
+        scaled_cos = high_cos[:, part : part + 1]
+        scaled_sin = high_sin[:, part : part + 1]
+        matrix[0:slots, columns] = (scaled_cos * low_cos - scaled_sin * low_sin).astype(jnp.bfloat16)
+        matrix[slots : 2 * slots, columns] = (-(scaled_sin * low_cos + scaled_cos * low_sin)).astype(
+            jnp.bfloat16
+        )
+    out_ref[...] = lax.dot_general(
+        matrix[...], grid_ref[...], (((1,), (1,)), ((), ())), preferred_element_type=jnp.float32
+    ).astype(jnp.bfloat16)
+
+
+def transform(grid_low, waves, lon_count):
+    groups, slots = waves.shape
+    wave_column = jnp.where(waves >= 0, waves, 0).reshape(1, groups * slots, 1)
+    step = jnp.arange(2, dtype=jnp.int32).reshape(2, 1, 1) * (LANES - 1) + 1
+    lane = lax.broadcasted_iota(jnp.int32, (1, 1, LANES), 2)
+    turns = (wave_column * ((step * lane) % lon_count)) % lon_count
+    angles = turns.astype(jnp.float32) * (2.0 * math.pi / lon_count)
+    scale = jnp.array([1.0, 1.0 / math.sqrt(lon_count)], jnp.float32).reshape(2, 1, 1)
+    tables = jnp.stack([jnp.cos(angles) * scale, jnp.sin(angles) * scale], axis=1)
+    tables = tables.reshape(4, groups * slots, LANES)
+    rows = grid_low.shape[0]
+    return pl.pallas_call(
+        functools.partial(transform_kernel, lon_count),
+        out_shape=jax.ShapeDtypeStruct((groups * 2 * slots, rows), jnp.bfloat16),
+        grid=(groups,),
+        in_specs=[
+            pl.BlockSpec((4, slots, LANES), lambda g: (0, g, 0)),
+            pl.BlockSpec((rows, lon_count), lambda g: (0, 0)),
+        ],
+        out_specs=pl.BlockSpec((2 * slots, rows), lambda g: (g, 0)),
+        scratch_shapes=[pltpu.VMEM((2 * slots, lon_count), jnp.bfloat16)],
+        compiler_params=pltpu.CompilerParams(vmem_limit_bytes=32 << 20),
+    )(tables, grid_low)
+
+
+def exchange_kernel(lat_size, fld_size, rep_size, source, target, send_sem, recv_sem, own_sem):
+    lat, fld, rep = lax.axis_index("lat"), lax.axis_index("fld"), lax.axis_index("rep")
+    groups = lat_size * fld_size
+    rows = target.shape[1]
+    half = fld_size // rep_size
+    to_rep = fld // half
+    place = ((fld % half) * lat_size + lat) * rep_size + rep
+    own = lat * fld_size + fld
+    stays = to_rep == rep
+
+    def sending(hop):
+        group = (own + hop) % groups
+        return pltpu.make_async_remote_copy(
+            src_ref=source.at[pl.ds(pl.multiple_of(group * rows, 16), rows)],
+            dst_ref=target.at[place],
+            send_sem=send_sem.at[hop],
+            recv_sem=recv_sem.at[place],
+            device_id=(group // fld_size, group % fld_size, to_rep),
+            device_id_type=pl.DeviceIdType.MESH,
+        )
+
+    kept = pltpu.make_async_copy(
+        source.at[pl.ds(pl.multiple_of(own * rows, 16), rows)], target.at[place], own_sem
+    )
+    for hop in range(1, groups):
+        sending(hop).start()
+
+    @pl.when(stays)
+    def _():
+        kept.start()
+
+    @pl.when(jnp.logical_not(stays))
+    def _():
+        sending(0).start()
+
+    @pl.when(stays)
+    def _():
+        kept.wait()
+
+    @pl.when(jnp.logical_not(stays))
+    def _():
+        sending(0).wait_send()
+
+    for hop in range(1, groups):
+        sending(hop).wait_send()
+    for origin in range(target.shape[0]):
+
+        @pl.when(jnp.logical_not(stays & (place == origin)))
+        def _():
+            pltpu.make_async_remote_copy(
+                src_ref=target.at[origin],
+                dst_ref=target.at[origin],
+                send_sem=send_sem.at[0],
+                recv_sem=recv_sem.at[origin],
+                device_id=(lat, fld, 1 - rep),
+                device_id_type=pl.DeviceIdType.MESH,
+            ).wait_recv()
+
+
+def exchange(spectra, lat_size, fld_size, rep_size):
+    rows = spectra.shape[0] // (lat_size * fld_size)
+    origins = fld_size // rep_size * lat_size * rep_size
+    return pl.pallas_call(
+        functools.partial(exchange_kernel, lat_size, fld_size, rep_size),
+        out_shape=jax.ShapeDtypeStruct((origins, rows, spectra.shape[1]), spectra.dtype),
+        in_specs=[pl.BlockSpec(memory_space=pltpu.VMEM)],
+        out_specs=pl.BlockSpec(memory_space=pltpu.VMEM),
+        scratch_shapes=[
+            pltpu.SemaphoreType.DMA((lat_size * fld_size,)),
+            pltpu.SemaphoreType.DMA((origins,)),
+            pltpu.SemaphoreType.DMA,
+        ],
+        compiler_params=pltpu.CompilerParams(has_side_effects=True, vmem_limit_bytes=16 << 20),
+    )(spectra)
+
+
+def legendre_kernel(
+    bands, field_count, first, last, received, starts, stops, legendre, out, ordered, total
+):
+    slots = starts.shape[0]
+    row_count = received.shape[2] // field_count
+    tile = pl.program_id(0)
+    width = out.shape[3]
+
+    @pl.when(tile == 0)
+    def _():
+        for origin in range(received.shape[0]):
+            part, band = divmod(origin, bands)
+            for level in range(field_count):
+                for side in range(2):
+                    row = (part * field_count + level) * 2 + side
+                    ordered[row, :, band * row_count : (band + 1) * row_count] = received[
+                        origin,
+                        side * slots : (side + 1) * slots,
+                        level * row_count : (level + 1) * row_count,
+                    ]
+
+    total[...] = jnp.zeros_like(total)
+    rows = ordered.shape[0]
+
+    @pl.loop(first[tile], last[tile])
+    def _(window):
+        here = pl.ds(pl.multiple_of(window * WINDOW, WINDOW), WINDOW)
+        products = jnp.dot(
+            ordered[:, here, :].reshape(rows * WINDOW, ordered.shape[2]),
+            legendre[0],
+            preferred_element_type=jnp.float32,
+        ).reshape(rows, WINDOW, width)
+        columns = tile * width + lax.broadcasted_iota(jnp.int32, (WINDOW, width), 1)
+        held = (columns >= starts[here, :]) & (columns < stops[here, :])
+        total[...] += jnp.sum(jnp.where(held[None], products, 0.0), axis=1)
+
+    for level in range(rows // 2):
+        out[0, level] = total[2 * level : 2 * level + 2, :]
+
+
+def legendre_sums(received, own_waves, legendre, field_count, bands, wave_total):
+    slots = own_waves.shape[0]
+    counts = jnp.where(own_waves >= 0, wave_total - own_waves, 0)
+    lower = lax.broadcasted_iota(jnp.int32, (slots, slots), 1) <= lax.broadcasted_iota(
+        jnp.int32, (slots, slots), 0
+    )
+    stops = jnp.sum(jnp.where(lower, counts[None, :], 0), axis=1)
+    starts = stops - counts
+    depth, col_count = legendre.shape[1:]
+    width = min(TILE, col_count)
+    tiles = pl.cdiv(col_count, width)
+    edges = jnp.arange(tiles, dtype=jnp.int32)[:, None] * width
+    first = jnp.sum((stops[None, :] <= edges).astype(jnp.int32), axis=1) // WINDOW
+    begun = jnp.sum((starts[None, :] < edges + width).astype(jnp.int32), axis=1)
+    last = (begun + WINDOW - 1) // WINDOW
+    rows = received.shape[0] // bands * field_count * 2
+    return pl.pallas_call(
+        functools.partial(legendre_kernel, bands, field_count),
+        out_shape=jax.ShapeDtypeStruct((1, rows // 2, 2, col_count), jnp.float32),
+        grid_spec=pltpu.PrefetchScalarGridSpec(
+            num_scalar_prefetch=2,
+            grid=(tiles,),
+            in_specs=[
+                pl.BlockSpec(
+                    received.shape, lambda t, *_: (0, 0, 0), pipeline_mode=pl.Buffered(1)
+                ),
+                pl.BlockSpec((slots, 1), lambda t, *_: (0, 0)),
+                pl.BlockSpec((slots, 1), lambda t, *_: (0, 0)),
+                pl.BlockSpec((1, depth, width), lambda t, *_: (0, 0, t)),
+            ],
+            out_specs=pl.BlockSpec((1, rows // 2, 2, width), lambda t, *_: (0, 0, 0, t)),
+            scratch_shapes=[
+                pltpu.VMEM((rows, slots, depth), jnp.bfloat16),
+                pltpu.VMEM((rows, width), jnp.float32),
+            ],
+        ),
+        compiler_params=pltpu.CompilerParams(vmem_limit_bytes=48 << 20),
+    )(first, last, received, starts[:, None], stops[:, None], legendre)
+
+
 def body(field, wind_zonal, wind_merid, band, waves, legendre):
     field_count, row_count, lon_count = field.shape
     lat_size = lax.axis_size("lat")
@@ -69,13 +273,31 @@
         )
     )
     grid_low = advected.astype(jnp.bfloat16)
+    slot_count = waves.shape[1]
+    direct = (
+        row_count % 16 == 0
+        and slot_count % WINDOW == 0
+        and lon_count % LANES == 0
+        and lon_count // LANES <= LANES
+        and fld_size % rep_size == 0
+        and lat_size * fld_size <= 64
+    )
+    if direct:
+        spectra = transform(
+            grid_low.reshape(field_count * row_count, lon_count), waves, lon_count
+        )
+        received = exchange(spectra, lat_size, fld_size, rep_size)
+        group = lax.axis_index("lat") * fld_size + lax.axis_index("fld")
+        own_waves = lax.dynamic_index_in_dim(waves, group, 0, keepdims=False)
+        return legendre_sums(
+            received, own_waves, legendre, field_count, lat_size * rep_size, M
+        )
     spectra = jnp.dot(
         grid_low.reshape(field_count * row_count, lon_count),
         dft_matrix(lon_count, M),
         preferred_element_type=jnp.float32,
     ).astype(jnp.bfloat16)
     spectra = spectra.reshape(field_count, row_count, 2, M)
-    slot_count = waves.shape[1]
     wave_index = jnp.where(waves >= 0, waves, 0)
     picked = jnp.take(spectra, wave_index.reshape(-1), axis=3)
     picked = picked.reshape(field_count, row_count, 2, lat_size, fld_size, slot_count)

time: 504 us -> 221 us (0.44)
  the two profiles are of different devices: /device:TPU:0 before, /device:TPU:15 now
where the time goes in v1:
time: 221 us; the launch traced here: 219 us
  Pallas kernels  162 us (73%)
  other arithmetic  28.7 us (13%)
  local copies, waits for them, and re-layouts  16 us (7%)
  starting transfers between devices  11.4 us (5%)
    pallas_call x1, Pallas kernels, exchange(): pl.pallas_call(functools.partial(exchange_kernel, lat_size, fld_size, rep...  74.1 us
    pallas_call x1, Pallas kernels, legendre_sums(): pl.pallas_call(functools.partial(legendre_kernel, bands, field_count), ou...  71.8 us
    pallas_call x1, Pallas kernels, transform(): pl.pallas_call(functools.partial(transform_kernel, lon_count), out_shape=...  16.5 us
    slice x4, local copies, waits for them, and re-layouts, tendency(): westward = jnp.roll(centre, 1, axis=-1)  14.5 us
    add x1, other arithmetic, body(): field + in_band * tendency(field, padded[:, 2:], padded[:, :-2], wind_zon...  13.8 us
    convert_element_type x1, other arithmetic, body(): grid_low = advected.astype(jnp.bfloat16)  8.65 us
    ppermute x2, starting transfers between devices, with_halo(): before = lax.ppermute(last, axis, up)  6.92 us
    mul x1, other arithmetic, transform(): jnp.cos(angles) * scale  5.4 us
  transfers between devices with their start and end apart: 4, of which 1 were waited for; matrix products, arithmetic and copies ran while one was open for 8% of the time, Pallas kernels for 0%

profile of v1, /device:TPU:15, one launch (start us, length us, event | category | flops | bytes accessed | tf_op | source)
XLA Modules:
  0.0 219.4 jit_solution(3965094048884714262)
XLA Ops:
  0.0 0.0 copy-start
  0.0 1.1 fusion.29
  1.1 2.6 %collective-permute-start = (f32[3,1,2560]{2,1,0:T(1,128)S(1)}, f32[3,1,2560]{2,1,0:T(1,128)S(1)}, u32[]{:S(2)}, u32[]{:S(2)}) collective-permute-start(f32[3,1,2560]{2,1,0:T(1,128)S(1)} %get-tuple-element.15), channel_id=1, source_target_pairs={{1,0},{8,1},{9,8},{16,9},{17,16},{24,17},{25,24},{3,2},{10,3},{11,... | collective-permute-start | bytes 92168 | tf_op jit(solution)/shard_map/ppermute | solution.py:25
  3.7 3.1 %collective-permute-start.1 = (f32[3,1,2560]{2,1,0:T(1,128)S(1)}, f32[3,1,2560]{2,1,0:T(1,128)S(1)}, u32[]{:S(2)}, u32[]{:S(2)}) collective-permute-start(f32[3,1,2560]{2,1,0:T(1,128)S(1)} %get-tuple-element.16), channel_id=1, source_target_pairs={{0,1},{1,8},{8,9},{9,16},{16,17},{17,24},{24,25},{2,3},{3,10},{10,... | collective-permute-start | bytes 92168 | tf_op jit(solution)/shard_map/ppermute | solution.py:24
  6.8 0.0 copy-start.1
  6.8 0.0 copy-start.2
  6.9 9.0 %fusion.28 = (f32[3,160,2559]{2,1,0:T(8,128)}, f32[3,160,2559]{2,1,0:T(8,128)}) fusion(f32[3,160,2560]{2,1,0:T(8,128)} %param.7), kind=kLoop, calls=%fused_computation.64 | loop fusion | bytes 19653120 | tf_op jit(solution)/shard_map/jit(_roll_static)/slice | solution.py:42
  15.9 1.2 fusion.27
  17.1 0.1 constant_dynamic-slice_fusion
  17.2 0.1 mul.165
  17.3 0.1 and_select_fusion
  17.4 0.1 select_reduce_fusion
  17.5 0.2 convert_reduce_fusion.1
  17.7 5.4 %cosine_multiply_fusion = (f32[2,1,1280,128]{3,2,1,0:T(8,128)S(1)}, f32[2,1,1280,128]{3,2,1,0:T(8,128)S(1)}) fusion(f32[2]{0:T(128)S(1)} %copy-done.2, s32[2,128]{1,0:T(2,128)S(1)} %and_select_fusion, s32[1280]{0:T(1024)S(1)} %mul.165), kind=kLoop, calls=%fused_computation.29 | loop fusion | flops 3604480 | bytes 2627592 | tf_op jit(solution)/shard_map/mul | solution.py:81
  23.1 0.2 pad_maximum_fusion.4
  23.3 0.2 convert_reduce_fusion
  23.5 0.1 and_convert_fusion
  23.6 0.1 copy.14.starts
  23.7 0.1 copy.15.stops
  23.8 0.0 collective-permute-done
  23.8 0.0 collective-permute-done.1
  23.8 13.8 %fusion.13 = f32[3,160,2560]{2,1,0:T(8,128)S(1)} fusion(f32[3,160,2560]{2,1,0:T(8,128)} %param.7, f32[3,160,2560]{2,1,0:T(8,128)} %param.9, f32[3,1,2560]{2,1,0:T(1,128)S(1)} %collective-permute-done.1, f32[3,1,2560]{2,1,0:T(1,128)S(1)} %collective-permute-done, f32[3,160,1]{2,1,0:T(8,128)S(1)} %get-tuple-element.12, f32[3,160,2559]{2,1,0:T(8,128)} %get-tuple-element.14, ...), kind=kLoop, calls=%fused_computation.16 | loop fusion | flops 18432000 | bytes 29554560 | tf_op jit(solution)/shard_map/add | solution.py:263
  37.6 4.1 %fusion.25 = (f32[3,160,2559]{2,1,0:T(8,128)S(1)}, f32[3,160,2559]{2,1,0:T(8,128)}) fusion(f32[3,160,2560]{2,1,0:T(8,128)S(1)} %fusion.13), kind=kLoop, calls=%fused_computation.61 | loop fusion | bytes 19653120 | tf_op jit(solution)/shard_map/jit(_roll_static)/slice | solution.py:42
  41.8 1.9 collective-permute-start.2
  43.8 3.8 %collective-permute-start.3 = (f32[3,1,2560]{2,1,0:T(1,128)S(1)}, f32[3,1,2560]{2,1,0:T(1,128)S(1)}, u32[]{:S(2)}, u32[]{:S(2)}) collective-permute-start(f32[3,1,2560]{2,1,0:T(1,128)S(1)} %get-tuple-element.10), channel_id=1, source_target_pairs={{0,1},{1,8},{8,9},{9,16},{16,17},{17,24},{24,25},{2,3},{3,10},{10,... | collective-permute-start | bytes 92168 | tf_op jit(solution)/shard_map/ppermute | solution.py:24
  47.6 0.1 fusion.24
  47.7 0.0 collective-permute-done.2
  47.7 0.7 collective-permute-done.3
  48.4 8.7 %fusion.7 = bf16[3,160,2560]{2,1,0:T(8,128)(2,1)S(1)} fusion(f32[3,160,2560]{2,1,0:T(8,128)} %param.9, f32[3,160,2560]{2,1,0:T(8,128)S(1)} %fusion.13, f32[3,1,2560]{2,1,0:T(1,128)S(1)} %collective-permute-done.3, f32[3,1,2560]{2,1,0:T(1,128)S(1)} %collective-permute-done.2, f32[3,160,1]{2,1,0:T(8,128)S(1)} %get-tuple-element.6, ...), kind=kLoop, calls=%fused_computation.8 | loop fusion | flops 22118400 | bytes 32012160 | tf_op jit(solution)/shard_map/convert_element_type | solution.py:275
  57.1 16.5 %shard_map.73.source = bf16[2560,480]{1,0:T(8,128)(2,1)S(1)} custom-call(f32[4,1280,128]{2,1,0:T(8,128)S(1)} %bitcast.18, bf16[480,2560]{1,0:T(8,128)(2,1)S(1)} %bitcast.19), custom_call_target="tpu_custom_call" | custom-call | tf_op jit(solution)/shard_map/pallas_call | solution.py:84
  73.5 74.1 %shard_map.74.received = bf16[16,160,480]{2,1,0:T(8,128)(2,1)S(1)} custom-call(bf16[2560,480]{1,0:T(8,128)(2,1)S(1)} %shard_map.73.source), custom_call_target="tpu_custom_call" | custom-call | tf_op jit(solution)/shard_map/pallas_call | solution.py:160
  147.7 71.8 %shard_map.75 = f32[1,6,2,51328]{3,2,1,0:T(2,128)} custom-call(s32[51]{0:T(128)S(1)} %get-tuple-element.22.first, s32[51]{0:T(128)S(1)} %get-tuple-element.21.last, bf16[16,160,480]{2,1,0:T(8,128)(2,1)S(1)} %shard_map.74.received, s32[80,1]{1,0:T(8,128)S(1)} %copy.14.starts, s32[80,1]{1,0:T(8,128)S(1)} %copy.15.stops, bf16[1,1280,51328]{2,1,0:T(8,128)(2,1)} %legendre.1), custom_call_target="tpu_custom_call" | custom-call | tf_op jit(solution)/shard_map/pallas_call | solution.py:230
  (14 shorter events, 0.1 us)
Async XLA Ops:
  0.0 17.1 %copy-start = (s32[12,2]{0,1:T(2,128)S(1)}, s32[12,2]{0,1:T(2,128)}, u32[]{:S(2)}) copy-start(s32[12,2]{0,1:T(2,128)} %param.10) | copy-start | bytes 292
  1.1 22.7 %collective-permute-start = (f32[3,1,2560]{2,1,0:T(1,128)S(1)}, f32[3,1,2560]{2,1,0:T(1,128)S(1)}, u32[]{:S(2)}, u32[]{:S(2)}) collective-permute-start(f32[3,1,2560]{2,1,0:T(1,128)S(1)} %get-tuple-element.15), channel_id=1, source_target_pairs={{1,0},{8,1},{9,8},{16,9},{17,16},{24,17},{25,24},{3,2},{10,3},{11,... | collective-permute-start | bytes 92168 | tf_op jit(solution)/shard_map/ppermute | solution.py:25
  3.7 20.1 %collective-permute-start.1 = (f32[3,1,2560]{2,1,0:T(1,128)S(1)}, f32[3,1,2560]{2,1,0:T(1,128)S(1)}, u32[]{:S(2)}, u32[]{:S(2)}) collective-permute-start(f32[3,1,2560]{2,1,0:T(1,128)S(1)} %get-tuple-element.16), channel_id=1, source_target_pairs={{0,1},{1,8},{8,9},{9,16},{16,17},{17,24},{24,25},{2,3},{3,10},{10,... | collective-permute-start | bytes 92168 | tf_op jit(solution)/shard_map/ppermute | solution.py:24
  6.8 10.4 %copy-start.1 = (s32[16,80]{1,0:T(8,128)S(1)}, s32[16,80]{1,0:T(8,128)}, u32[]{:S(2)}) copy-start(s32[16,80]{1,0:T(8,128)} %param.11) | copy-start | bytes 15364
  6.8 10.9 %copy-start.2 = (f32[2]{0:T(128)S(1)}, f32[2]{0:T(128)}, u32[]{:S(2)}) copy-start(f32[2]{0:T(128)} %constant.85.clone) | copy-start | bytes 28
  41.8 5.9 %collective-permute-start.2 = (f32[3,1,2560]{2,1,0:T(1,128)S(1)}, f32[3,1,2560]{2,1,0:T(1,128)S(1)}, u32[]{:S(2)}, u32[]{:S(2)}) collective-permute-start(f32[3,1,2560]{2,1,0:T(1,128)S(1)} %get-tuple-element.9), channel_id=1, source_target_pairs={{1,0},{8,1},{9,8},{16,9},{17,16},{24,17},{25,24},{3,2},{10,3},{11,... | collective-permute-start | bytes 92168 | tf_op jit(solution)/shard_map/ppermute | solution.py:25
  43.8 4.6 %collective-permute-start.3 = (f32[3,1,2560]{2,1,0:T(1,128)S(1)}, f32[3,1,2560]{2,1,0:T(1,128)S(1)}, u32[]{:S(2)}, u32[]{:S(2)}) collective-permute-start(f32[3,1,2560]{2,1,0:T(1,128)S(1)} %get-tuple-element.10), channel_id=1, source_target_pairs={{0,1},{1,8},{8,9},{9,16},{16,17},{17,24},{24,25},{2,3},{3,10},{10,... | collective-permute-start | bytes 92168 | tf_op jit(solution)/shard_map/ppermute | solution.py:24

commit v2 on v1

--- a/solution.py
+++ b/solution.py
@@ -11,7 +11,9 @@
 M = 1280
 LANES = 128
 WINDOW = 16
-TILE = 1024
+TILE = 4096
+PAD = 8
+CHUNK = 16
 
 
 def with_halo(value, sides, width):
@@ -247,8 +249,101 @@
                 pltpu.VMEM((rows, width), jnp.float32),
             ],
         ),
-        compiler_params=pltpu.CompilerParams(vmem_limit_bytes=48 << 20),
+        compiler_params=pltpu.CompilerParams(vmem_limit_bytes=56 << 20),
     )(first, last, received, starts[:, None], stops[:, None], legendre)
+
+
+def advection_kernel(bounds, origin, field, zonal, merid, above, below, out, edges, padded, section):
+    level = pl.program_id(0)
+    rows = field.shape[1]
+    length = field.shape[2]
+    lower, upper, start = bounds[level, 0], bounds[level, 1], origin[0]
+
+    def masked_slope(first_row, centre, turned_east, turned_west, next_row, previous, zonal_wind, merid_wind):
+        row_ids = start + first_row + lax.broadcasted_iota(jnp.int32, centre.shape, 0)
+        in_band = ((row_ids >= lower) & (row_ids < upper)).astype(jnp.float32)
+        return in_band * (
+            -(zonal_wind + centre) * (turned_east - turned_west) * 0.5
+            - merid_wind * (next_row - previous) * 0.5
+        )
+
+    def turned(value):
+        return pltpu.roll(value, length - 1, axis=1), pltpu.roll(value, 1, axis=1)
+
+    padded[PAD : PAD + rows, :] = field[0]
+    padded[PAD - 2 : PAD, :] = above[0, 0:2, :]
+    padded[PAD + rows : PAD + rows + 2, :] = below[0, 0:2, :]
+    edges[0:4, :] = above[0]
+    edges[4:8, :] = below[0]
+    halo = edges[...]
+    east, west = turned(halo)
+    section[PAD - 1 : PAD, :] = halo[1:2] + masked_slope(
+        -1, halo[1:2], east[1:2], west[1:2], field[0, 0:1, :], halo[0:1], halo[2:3], halo[3:4]
+    )
+    section[PAD + rows : PAD + rows + 1, :] = halo[4:5] + masked_slope(
+        rows, halo[4:5], east[4:5], west[4:5], halo[5:6], field[0, rows - 1 : rows, :], halo[6:7], halo[7:8]
+    )
+
+    def neighbours(ref, first_row):
+        value = ref[pl.ds(first_row, 2 * PAD + CHUNK), :]
+        return tuple(value[PAD + shift : PAD + shift + CHUNK] for shift in (-1, 0, 1))
+
+    @pl.loop(0, rows // CHUNK)
+    def _(chunk):
+        first_row = pl.multiple_of(chunk * CHUNK, CHUNK)
+        here = pl.ds(first_row, CHUNK)
+        previous, centre, next_row = neighbours(padded, first_row)
+        section[pl.ds(pl.multiple_of(first_row + PAD, PAD), CHUNK), :] = centre + masked_slope(
+            first_row, centre, *turned(centre), next_row, previous, zonal[0, here, :], merid[0, here, :]
+        )
+
+    @pl.loop(0, rows // CHUNK)
+    def _(chunk):
+        first_row = pl.multiple_of(chunk * CHUNK, CHUNK)
+        here = pl.ds(first_row, CHUNK)
+        previous, centre, next_row = neighbours(section, first_row)
+        out[0, here, :] = (
+            0.5
+            * (
+                field[0, here, :]
+                + centre
+                + masked_slope(
+                    first_row, centre, *turned(centre), next_row, previous, zonal[0, here, :], merid[0, here, :]
+                )
+            )
+        ).astype(jnp.bfloat16)
+
+
+def advection(field, wind_zonal, wind_merid, bounds, first_row):
+    levels, rows, length = field.shape
+    peers = lax.axis_size(("lat", "rep"))
+    up = [(i, i + 1) for i in range(peers - 1)]
+    down = [(i + 1, i) for i in range(peers - 1)]
+    winds = (wind_zonal, wind_merid)
+    above = lax.ppermute(
+        jnp.concatenate([field[:, -2:]] + [w[:, -1:] for w in winds], axis=1), ("lat", "rep"), up
+    )
+    below = lax.ppermute(
+        jnp.concatenate([field[:, :2]] + [w[:, :1] for w in winds], axis=1), ("lat", "rep"), down
+    )
+    whole = pl.BlockSpec((1, rows, length), lambda f, *_: (f, 0, 0))
+    edge = pl.BlockSpec((1, 4, length), lambda f, *_: (f, 0, 0))
+    return pl.pallas_call(
+        advection_kernel,
+        out_shape=jax.ShapeDtypeStruct(field.shape, jnp.bfloat16),
+        grid_spec=pltpu.PrefetchScalarGridSpec(
+            num_scalar_prefetch=2,
+            grid=(levels,),
+            in_specs=[whole, whole, whole, edge, edge],
+            out_specs=whole,
+            scratch_shapes=[
+                pltpu.VMEM((8, length), jnp.float32),
+                pltpu.VMEM((rows + 2 * PAD, length), jnp.float32),
+                pltpu.VMEM((rows + 2 * PAD, length), jnp.float32),
+            ],
+        ),
+        compiler_params=pltpu.CompilerParams(vmem_limit_bytes=60 << 20),
+    )(bounds, first_row.reshape(1), field, wind_zonal, wind_merid, above, below)
 
 
 def body(field, wind_zonal, wind_merid, band, waves, legendre):
@@ -258,21 +353,6 @@
     rep_size = lax.axis_size("rep")
     first_row = (lax.axis_index("lat") * rep_size + lax.axis_index("rep")) * row_count
     bounds = lax.dynamic_slice_in_dim(band, lax.axis_index("fld") * field_count, field_count, 0)
-    in_band = band_mask(bounds, first_row, row_count)
-    padded = with_halo(field, ((("lat", "rep"), 1),), 1)
-    first_section = field + in_band * tendency(
-        field, padded[:, 2:], padded[:, :-2], wind_zonal, wind_merid
-    )
-    padded_section = with_halo(first_section, ((("lat", "rep"), 1),), 1)
-    advected = 0.5 * (
-        field
-        + first_section
-        + in_band
-        * tendency(
-            first_section, padded_section[:, 2:], padded_section[:, :-2], wind_zonal, wind_merid
-        )
-    )
-    grid_low = advected.astype(jnp.bfloat16)
     slot_count = waves.shape[1]
     direct = (
         row_count % 16 == 0
@@ -283,6 +363,7 @@
         and lat_size * fld_size <= 64
     )
     if direct:
+        grid_low = advection(field, wind_zonal, wind_merid, bounds, first_row)
         spectra = transform(
             grid_low.reshape(field_count * row_count, lon_count), waves, lon_count
         )
@@ -292,6 +373,21 @@
         return legendre_sums(
             received, own_waves, legendre, field_count, lat_size * rep_size, M
         )
+    in_band = band_mask(bounds, first_row, row_count)
+    padded = with_halo(field, ((("lat", "rep"), 1),), 1)
+    first_section = field + in_band * tendency(
+        field, padded[:, 2:], padded[:, :-2], wind_zonal, wind_merid
+    )
+    padded_section = with_halo(first_section, ((("lat", "rep"), 1),), 1)
+    advected = 0.5 * (
+        field
+        + first_section
+        + in_band
+        * tendency(
+            first_section, padded_section[:, 2:], padded_section[:, :-2], wind_zonal, wind_merid
+        )
+    )
+    grid_low = advected.astype(jnp.bfloat16)
     spectra = jnp.dot(
         grid_low.reshape(field_count * row_count, lon_count),
         dft_matrix(lon_count, M),

time: 221 us -> 187 us (0.85)
  other arithmetic: 28.7 us -> 10.4 us
  local copies, waits for them, and re-layouts: 16 us -> 8.64 us
  starting transfers between devices: 11.4 us -> 5.69 us
    pallas_call x1, Pallas kernels: 71.8 us -> 56.3 us  [legendre_sums(): pl.pallas_call(functools.partial(legendre_kernel, bands, field_count), ou...]
    pallas_call x0 -> x1, Pallas kernels: none -> 15.3 us  [advection(): pl.pallas_call(advection_kernel, out_shape=jax.ShapeDtypeStruct(field.sha...]
    add x2 -> x0, other arithmetic: 13.8 us -> none  [the longest x1 13.8 us: body(): field + in_band * tendency(field, padded[:, 2:], padded[:, :-2], wind_zon...]
    slice x7 -> x2, local copies, waits for them, and re-layouts: 15.7 us -> 2.52 us  [the longest x1 1.4 us: advection(): w[:, :1]]
    convert_element_type x2 -> x0, other arithmetic: 8.73 us -> none  [the longest x1 8.65 us: body(): grid_low = advected.astype(jnp.bfloat16)]
    ppermute x4 -> x2, starting transfers between devices: 11.4 us -> 5.69 us  [the longest x1 3.77 us: advection(): lax.ppermute(jnp.concatenate([field[:, -2:]] + [w[:, -1:] for w in winds]...]
    unnamed x6 -> x11, local copies, waits for them, and re-layouts: 0.02 us -> 4.55 us
  transfers between devices with their start and end apart: 4 -> 2, of which waited for: 1 -> 0; matrix products, arithmetic and copies ran while one was open for 8% -> 7% of each run, Pallas kernels for 0% -> 0%
where the time goes in v2:
time: 187 us; the launch traced here: 186 us
  Pallas kernels  161 us (86%)
  other arithmetic  10.4 us (6%)
  local copies, waits for them, and re-layouts  8.64 us (5%)
  starting transfers between devices  5.69 us (3%)
    pallas_call x1, Pallas kernels, exchange(): pl.pallas_call(functools.partial(exchange_kernel, lat_size, fld_size, rep...  73.5 us
    pallas_call x1, Pallas kernels, legendre_sums(): pl.pallas_call(functools.partial(legendre_kernel, bands, field_count), ou...  56.3 us
    pallas_call x1, Pallas kernels, transform(): pl.pallas_call(functools.partial(transform_kernel, lon_count), out_shape=...  16 us
    pallas_call x1, Pallas kernels, advection(): pl.pallas_call(advection_kernel, out_shape=jax.ShapeDtypeStruct(field.sha...  15.3 us
    mul x1, other arithmetic, transform(): jnp.cos(angles) * scale  6.06 us
    unnamed x11, local copies, waits for them, and re-layouts  4.55 us
    ppermute x1, starting transfers between devices, advection(): lax.ppermute(jnp.concatenate([field[:, -2:]] + [w[:, -1:] for w in winds]...  3.77 us
  transfers between devices with their start and end apart: 2, of which 0 were waited for; matrix products, arithmetic and copies ran while one was open for 7% of the time, Pallas kernels for 0%

profile of v2, /device:TPU:15, one launch (start us, length us, event | category | flops | bytes accessed | tf_op | source)
XLA Modules:
  0.0 186.0 jit_solution(5865267298916720872)
XLA Ops:
  0.0 1.1 fusion.6
  1.1 1.4 fusion.7
  2.5 0.1 pad_maximum_fusion.1
  2.6 3.8 %collective-permute-start = (f32[3,4,2560]{2,1,0:T(4,128)S(1)}, f32[3,4,2560]{2,1,0:T(4,128)S(1)}, u32[]{:S(2)}, u32[]{:S(2)}) collective-permute-start(f32[3,4,2560]{2,1,0:T(4,128)S(1)} %pad_maximum_fusion.1), channel_id=1, source_target_pairs={{0,1},{1,8},{8,9},{9,16},{16,17},{17,24},{24,25},{2,3},{3,10},{10,... | collective-permute-start | bytes 368648 | tf_op jit(solution)/shard_map/ppermute | solution.py:323
  6.4 0.1 pad_maximum_fusion.2
  6.5 1.9 %collective-permute-start.1 = (f32[3,4,2560]{2,1,0:T(4,128)S(1)}, f32[3,4,2560]{2,1,0:T(4,128)S(1)}, u32[]{:S(2)}, u32[]{:S(2)}) collective-permute-start(f32[3,4,2560]{2,1,0:T(4,128)S(1)} %pad_maximum_fusion.2), channel_id=1, source_target_pairs={{1,0},{8,1},{9,8},{16,9},{17,16},{24,17},{25,24},{3,2},{10,3},{11,... | collective-permute-start | bytes 368648 | tf_op jit(solution)/shard_map/ppermute | solution.py:326
  8.5 0.7 compare_select_fusion
  9.2 0.7 fusion.9
  9.9 0.1 select_reduce_fusion
  10.0 0.7 fusion.5
  10.7 0.7 bitcast_subtract_fusion
  11.4 0.2 convert_reduce_fusion.1
  11.5 0.1 and_select_fusion
  11.6 0.1 mul.124
  11.7 0.1 constant_dynamic-slice_fusion
  11.8 0.7 copy.19.bounds
  12.5 0.7 copy.17.starts
  13.2 0.7 copy.18.stops
  13.9 0.2 convert_reduce_fusion
  14.1 6.1 %cosine_multiply_fusion = (f32[2,1,1280,128]{3,2,1,0:T(8,128)S(1)}, f32[2,1,1280,128]{3,2,1,0:T(8,128)S(1)}) fusion(f32[2]{0:T(128)} %constant.83.clone, s32[2,128]{1,0:T(2,128)S(1)} %and_select_fusion, s32[1280]{0:T(1024)S(1)} %mul.124), kind=kLoop, calls=%fused_computation.5 | loop fusion | flops 3604480 | bytes 2627592 | tf_op jit(solution)/shard_map/mul | solution.py:83
  20.1 0.2 pad_maximum_fusion
  20.3 0.6 and_select_fusion.1
  20.9 0.0 collective-permute-done.above
  20.9 0.0 collective-permute-done.1.below
  20.9 0.6 copy-done.3
  21.6 0.0 copy-done.4
  21.6 15.3 %shard_map.73 = bf16[3,160,2560]{2,1,0:T(8,128)(2,1)} custom-call(s32[3,2]{1,0:T(4,128)} %copy.19.bounds, s32[1]{0:T(128)} %bitcast.4.origin, f32[3,160,2560]{2,1,0:T(8,128)} %field.1, f32[3,160,2560]{2,1,0:T(8,128)} %zonal.1, f32[3,160,2560]{2,1,0:T(8,128)} %merid.1, f32[3,4,2560]{2,1,0:T(4,128)} %copy-done.3, f32[3,4,2560]{2,1,0:T(4,128)} %copy-done.4), custom_call_target="tpu_custom_call" | custom-call | tf_op jit(solution)/shard_map/pallas_call | solution.py:331
  36.9 1.7 copy-done.2
  38.6 16.0 %shard_map.74.source = bf16[2560,480]{1,0:T(8,128)(2,1)S(1)} custom-call(f32[4,1280,128]{2,1,0:T(8,128)S(1)} %bitcast.15, bf16[480,2560]{1,0:T(8,128)(2,1)S(1)} %bitcast.16), custom_call_target="tpu_custom_call" | custom-call | tf_op jit(solution)/shard_map/pallas_call | solution.py:86
  54.6 73.5 %shard_map.75.received = bf16[16,160,480]{2,1,0:T(8,128)(2,1)S(1)} custom-call(bf16[2560,480]{1,0:T(8,128)(2,1)S(1)} %shard_map.74.source), custom_call_target="tpu_custom_call" | custom-call | tf_op jit(solution)/shard_map/pallas_call | solution.py:162
  128.1 1.5 copy-done.1
  129.6 56.3 %shard_map.76 = f32[1,6,2,51328]{3,2,1,0:T(2,128)} custom-call(s32[13]{0:T(128)} %get-tuple-element.14.first, s32[13]{0:T(128)} %get-tuple-element.13.last, bf16[16,160,480]{2,1,0:T(8,128)(2,1)} %copy-done.1, s32[80,1]{1,0:T(8,128)} %copy.17.starts, s32[80,1]{1,0:T(8,128)} %copy.18.stops, bf16[1,1280,51328]{2,1,0:T(8,128)(2,1)} %legendre.1), custom_call_target="tpu_custom_call" | custom-call | tf_op jit(solution)/shard_map/pallas_call | solution.py:232
  (9 shorter events, 0.0 us)
Async XLA Ops:
  0.0 11.7 %copy-start = (s32[12,2]{0,1:T(2,128)S(1)}, s32[12,2]{0,1:T(2,128)}, u32[]{:S(2)}) copy-start(s32[12,2]{0,1:T(2,128)} %param.10) | copy-start | bytes 292
  2.6 18.3 %collective-permute-start = (f32[3,4,2560]{2,1,0:T(4,128)S(1)}, f32[3,4,2560]{2,1,0:T(4,128)S(1)}, u32[]{:S(2)}, u32[]{:S(2)}) collective-permute-start(f32[3,4,2560]{2,1,0:T(4,128)S(1)} %pad_maximum_fusion.1), channel_id=1, source_target_pairs={{0,1},{1,8},{8,9},{9,16},{16,17},{17,24},{24,25},{2,3},{3,10},{10,... | collective-permute-start | bytes 368648 | tf_op jit(solution)/shard_map/ppermute | solution.py:323
  6.5 14.4 %collective-permute-start.1 = (f32[3,4,2560]{2,1,0:T(4,128)S(1)}, f32[3,4,2560]{2,1,0:T(4,128)S(1)}, u32[]{:S(2)}, u32[]{:S(2)}) collective-permute-start(f32[3,4,2560]{2,1,0:T(4,128)S(1)} %pad_maximum_fusion.2), channel_id=1, source_target_pairs={{1,0},{8,1},{9,8},{16,9},{17,16},{24,17},{25,24},{3,2},{10,3},{11,... | collective-permute-start | bytes 368648 | tf_op jit(solution)/shard_map/ppermute | solution.py:326
  20.9 0.6 copy-start.3
  20.9 0.7 copy-start.4
  36.9 1.7 copy-start.2
  128.1 1.5 copy-start.1
